TPU v7x, 128 devices: a whole 4x4x4 slice. The times are simulated.
128 devices in a mesh: row: 16 (over x, y_lo, core), col: 8 (over y_hi, z).
Axes of the slice: x: 4, y: 4 (y_hi: 2, y_lo: 2; y = y_hi * 2 + y_lo), z: 4, core: 2. Of those that a mesh axis runs over, the one named last changes fastest.
Arguments:
- weight: bfloat16 [6144, 6144], P('row', 'col'), may hold values from -6 to 6
- right_op: bfloat16 [8192, 6144], P('row', 'col'), may hold values from -0.078125 to 0.078125
- left_op: bfloat16 [8192, 6144], P('row', 'col'), may hold values from -0.078125 to 0.078125
Outputs:
- grown: bfloat16 [8192, 8192], P(('row', 'col'))
All inputs are finite; a program needn't handle non-finite values.
Results may differ from a plain program's by a relative error of at most 0.018.
Values may be sent and summed in bfloat16 or wider, within the bound.
No kernel may reach another device: no remote copies, remote signals or barrier semaphores. Data moves between devices by JAX's collectives and lax.ppermute only.
A program may use at most 64 MiB of HBM per device.

v0:
```python
import jax
import jax.numpy as jnp
from jax import lax
from jax.sharding import PartitionSpec as P


def split_up(x, dim, size):
    shape = x.shape
    pieces = x.reshape(*shape[:dim], size, shape[dim] // size, *shape[dim + 1 :])
    return jnp.moveaxis(pieces, dim, 0)


def sum_at_owner(x, axis, dim):
    size = lax.axis_size(axis)
    pieces = lax.all_to_all(split_up(x, dim, size), axis, 0, 0, tiled=True)
    return jnp.sum(pieces.astype(jnp.float32), axis=0)


def round_terms(values):
    return lax.optimization_barrier(values.astype(jnp.bfloat16)).astype(jnp.float32)


def shards(weight, right_op, left_op):
    weight_whole = lax.all_gather(weight, "row", axis=0, tiled=True)
    partial_value = jnp.einsum(
        "ik,jk->ij", weight_whole, right_op, preferred_element_type=jnp.float32
    )
    middle = sum_at_owner(round_terms(partial_value).astype(jnp.bfloat16), "col", 0).astype(
        jnp.bfloat16
    )
    terms = jnp.dot(
        left_op,
        lax.all_gather(middle, "row", axis=1, tiled=True),
        preferred_element_type=jnp.float32,
    )
    return lax.psum_scatter(
        round_terms(terms).astype(jnp.bfloat16), "col", scatter_dimension=0, tiled=True
    )


def solution(mesh):
    in_specs = (P("row", "col"), P("row", "col"), P("row", "col"))
    out_specs = P(("row", "col"), None)
    return jax.shard_map(shards, mesh=mesh, in_specs=in_specs, out_specs=out_specs, check_vma=False)
```

profile of v0, /device:TPU:0, one launch (start us, length us, event | category | flops | bytes accessed | tf_op | source)
XLA Modules:
  0.0 379.2 jit_solution(7308006104932658179)
XLA Ops:
  6.5 0.0 copy-start
  6.5 0.0 all-gather.3.cloned.1.call-start
  6.5 0.7 all-gather.3.cloned.1.call-update
  7.3 0.0 all-gather.5.cloned.1.call-start
  7.3 61.2 %all-gather.3.cloned.1.call-done = bf16[6144,768]{1,0:T(8,128)(2,1)} async-done(((bf16[384,768]{1,0:T(8,128)(2,1)}), bf16[6144,768]{1,0:T(8,128)(2,1)}) %all-gather.3.cloned.1.call-update) | async-done | bytes 9437200 | tf_op jit(solution)/shard_map/all_gather | solution.py:24
  68.5 9.2 %convolution_convert_fusion.1 = bf16[6144,512]{1,0:T(8,128)(2,1)S(1)} fusion(bf16[6144,768]{1,0:T(8,128)(2,1)} %all-gather.3.cloned.1.call-done, bf16[512,768]{1,0:T(8,128)(2,1)} %param.4), kind=kOutput, calls=%fused_computation.2 | convolution fusion | flops 4834983936 | bytes 16515072 | tf_op jit(solution)/shard_map/ik,jk->ij/dot_general | solution.py:25
  77.7 80.4 %all_to_all.5 = bf16[8,768,512]{2,1,0:T(8,128)(2,1)} all-to-all(bf16[8,768,512]{2,1,0:T(8,128)(2,1)S(1)} %bitcast.8), channel_id=1, replica_groups=mesh['row'=16,'col'=8] {'col'}, dimensions={0} | all-to-all | bytes 12582912 | tf_op jit(solution)/shard_map/all_to_all | solution.py:15
  158.1 4.8 %reduce_sum.12 = bf16[768,512]{1,0:T(8,128)(2,1)} reduce(bf16[8,768,512]{2,1,0:T(8,128)(2,1)} %all_to_all.5, bf16[]{:T(256)} %constant.2.clone.1), dimensions={0}, to_apply=%region_0.0 | reduce | flops 2752512 | bytes 7077890 | tf_op jit(solution)/shard_map/reduce_sum | solution.py:16
  162.9 0.0 all-gather.5.cloned.1.call-update
  162.9 0.0 reduce-scatter.4.cloned.1.call-start
  163.0 68.8 %all-gather.5.cloned.1.call-done = bf16[768,8192]{1,0:T(8,128)(2,1)} async-done(((bf16[768,512]{1,0:T(8,128)(2,1)}), bf16[768,8192]{1,0:T(8,128)(2,1)}) %all-gather.5.cloned.1.call-update) | async-done | bytes 12582928 | tf_op jit(solution)/shard_map/all_gather | solution.py:33
  231.7 0.0 copy-done
  231.7 13.6 %fusion = bf16[512,8192]{0,1:T(8,128)(2,1)} fusion(bf16[768,8192]{1,0:T(8,128)(2,1)} %all-gather.5.cloned.1.call-done, bf16[512,768]{1,0:T(8,128)(2,1)S(1)} %copy-done), kind=kOutput, calls=%fused_computation.1 | convolution fusion | flops 6446645248 | bytes 21757952 | tf_op jit(solution)/shard_map/dot_general | solution.py:31
  245.4 11.9 %copy.6 = bf16[512,8192]{1,0:T(8,128)(2,1)} copy(bf16[512,8192]{0,1:T(8,128)(2,1)} %fusion) | data formatting | bytes 16777216
  257.2 0.0 reduce-scatter.4.cloned.1.call-update
  257.3 115.4 %reduce-scatter.4.cloned.1.call-done = bf16[64,8192]{1,0:T(8,128)(2,1)} async-done(((bf16[512,8192]{1,0:T(8,128)(2,1)}), bf16[64,8192]{1,0:T(8,128)(2,1)}) %reduce-scatter.4.cloned.1.call-update) | async-done | bytes 1048592 | tf_op jit(solution)/shard_map/reduce_scatter | solution.py:36
Async XLA Ops:
  6.5 225.2 %copy-start = (bf16[512,768]{1,0:T(8,128)(2,1)S(1)}, bf16[512,768]{1,0:T(8,128)(2,1)}, u32[]{:S(2)}) copy-start(bf16[512,768]{1,0:T(8,128)(2,1)} %param.5) | copy-start | bytes 2359300
  6.5 62.0 %all-gather.3.cloned.1.call-start = ((), (), s32[]{:S(2)}) async-start(), calls=%async_computation.2 | async-start | bytes 10027008 | tf_op jit(solution)/shard_map/all_gather | solution.py:24
  7.3 224.5 %all-gather.5.cloned.1.call-start = ((), (), s32[]{:S(2)}) async-start(), calls=%async_computation.3 | async-start | bytes 13369344 | tf_op jit(solution)/shard_map/all_gather | solution.py:33
  162.9 209.8 %reduce-scatter.4.cloned.1.call-start = ((), (), s32[]{:S(2)}) async-start(), calls=%async_computation.4 | async-start | bytes 9437184 | tf_op jit(solution)/shard_map/reduce_scatter | solution.py:36
Sparse Core Ops, SparseCore 0:
  9.0 59.4 all-gather.2
  163.0 68.6 all-gather.4
  257.4 115.2 reduce-scatter.3
where the time goes:
time: 380 us; the launch traced here: 379 us
  waiting for transfers between devices  246 us (65%)
  blocking collectives  80.4 us (21%)
  matrix products  22.8 us (6%)
  between operations  13.1 us (3%)
  local copies, waits for them, and re-layouts  11.9 us (3%)
  other arithmetic  4.79 us (1%)
    reduce_scatter x1, waiting for transfers between devices, shards(): lax.psum_scatter(round_terms(terms).astype(jnp.bfloat16), 'col', scatter_...  115 us
    all_to_all x1, blocking collectives, sum_at_owner(): pieces = lax.all_to_all(split_up(x, dim, size), axis, 0, 0, tiled=True)  80.4 us
    all_gather x1, waiting for transfers between devices, shards(): lax.all_gather(middle, 'row', axis=1, tiled=True)  68.8 us
    all_gather x1, waiting for transfers between devices, shards(): weight_whole = lax.all_gather(weight, 'row', axis=0, tiled=True)  61.2 us
    dot_general x1, matrix products, shards(): jnp.dot(left_op, lax.all_gather(middle, 'row', axis=1, tiled=True), prefe...  13.6 us
    unnamed x3, local copies, waits for them, and re-layouts  11.9 us
    dot_general x1, matrix products, shards(): jnp.einsum('ik,jk->ij', weight_whole, right_op, preferred_element_type=jn...  9.17 us
  transfers between devices with their start and end apart: 3, of which 3 were waited for; matrix products, arithmetic and copies ran while one was open for 0% of the time, Pallas kernels for 0%

commit v1 on v0

--- a/solution.py
+++ b/solution.py
@@ -2,6 +2,13 @@
 import jax.numpy as jnp
 from jax import lax
 from jax.sharding import PartitionSpec as P
+
+
+def swapped_in(shard, name, dim):
+    size = lax.axis_size(name)
+    tiles = jnp.stack([shard for _ in range(size)])
+    tiles = lax.all_to_all(tiles, name, split_axis=0, concat_axis=0)
+    return jnp.concatenate(tiles, axis=dim)
 
 
 def split_up(x, dim, size):
@@ -28,11 +35,7 @@
     middle = sum_at_owner(round_terms(partial_value).astype(jnp.bfloat16), "col", 0).astype(
         jnp.bfloat16
     )
-    terms = jnp.dot(
-        left_op,
-        lax.all_gather(middle, "row", axis=1, tiled=True),
-        preferred_element_type=jnp.float32,
-    )
+    terms = jnp.dot(left_op, swapped_in(middle, "row", 1), preferred_element_type=jnp.float32)
     return lax.psum_scatter(
         round_terms(terms).astype(jnp.bfloat16), "col", scatter_dimension=0, tiled=True
     )

time: 380 us -> 452 us (1.19)
  blocking collectives: 80.4 us -> 225 us
  waiting for transfers between devices: 246 us -> 173 us
  local copies, waits for them, and re-layouts: 11.9 us -> 18.1 us
    all_to_all x0 -> x1, blocking collectives: none -> 144 us  [swapped_in(): tiles = lax.all_to_all(tiles, name, split_axis=0, concat_axis=0)]
    all_gather x1 -> x0, waiting for transfers between devices: 68.8 us -> none  [shards(): lax.all_gather(middle, 'row', axis=1, tiled=True)]
    another operation x0 -> x1, local copies, waits for them, and re-layouts: none -> 5.78 us  [swapped_in(): tiles = jnp.stack([shard for _ in range(size)])]
  transfers between devices with their start and end apart: 3 -> 2, of which waited for: 3 -> 2; matrix products, arithmetic and copies ran while one was open for 0% -> 0% of each run, Pallas kernels for 0% -> 0%
where the time goes in v1:
time: 452 us
  blocking collectives  225 us (50%)
  waiting for transfers between devices  173 us (38%)
  matrix products  18.3 us (4%)
  local copies, waits for them, and re-layouts  18.1 us (4%)
  between operations  13.4 us (3%)
    all_to_all x1, blocking collectives, swapped_in(): tiles = lax.all_to_all(tiles, name, split_axis=0, concat_axis=0)  144 us
    reduce_scatter x1, waiting for transfers between devices, shards(): lax.psum_scatter(round_terms(terms).astype(jnp.bfloat16), 'col', scatter_...  111 us
    all_to_all x1, blocking collectives, sum_at_owner(): pieces = lax.all_to_all(split_up(x, dim, size), axis, 0, 0, tiled=True)  80.4 us
    all_gather x1, waiting for transfers between devices, shards(): weight_whole = lax.all_gather(weight, 'row', axis=0, tiled=True)  61.2 us
    unnamed x3, local copies, waits for them, and re-layouts  12 us
    dot_general x1, matrix products, shards(): jnp.einsum('ik,jk->ij', weight_whole, right_op, preferred_element_type=jn...  9.17 us
    dot_general x1, matrix products, shards(): jnp.dot(left_op, swapped_in(middle, 'row', 1), preferred_element_type=jnp...  9.15 us
  transfers between devices with their start and end apart: 2, of which 2 were waited for; matrix products, arithmetic and copies ran while one was open for 0% of the time, Pallas kernels for 0%

profile of v1, /device:TPU:0, one launch (start us, length us, event | category | flops | bytes accessed | tf_op | source)
XLA Modules:
  0.0 451.8 jit_solution(13155819684709232751)
XLA Ops:
  6.5 0.0 copy-start
  6.5 0.0 all-gather.2.cloned.1.call-start
  6.5 0.7 all-gather.2.cloned.1.call-update
  7.3 0.0 reduce-scatter.4.cloned.1.call-start
  7.3 61.2 %all-gather.2.cloned.1.call-done = bf16[6144,768]{1,0:T(8,128)(2,1)} async-done(((bf16[384,768]{1,0:T(8,128)(2,1)}), bf16[6144,768]{1,0:T(8,128)(2,1)}) %all-gather.2.cloned.1.call-update) | async-done | bytes 9437200 | tf_op jit(solution)/shard_map/all_gather | solution.py:31
  68.5 9.2 %convolution_convert_fusion.1 = bf16[6144,512]{1,0:T(8,128)(2,1)S(1)} fusion(bf16[6144,768]{1,0:T(8,128)(2,1)} %all-gather.2.cloned.1.call-done, bf16[512,768]{1,0:T(8,128)(2,1)} %param.4), kind=kOutput, calls=%fused_computation.2 | convolution fusion | flops 4834983936 | bytes 16515072 | tf_op jit(solution)/shard_map/ik,jk->ij/dot_general | solution.py:32
  77.7 80.4 %all_to_all.10 = bf16[8,768,512]{2,1,0:T(8,128)(2,1)} all-to-all(bf16[8,768,512]{2,1,0:T(8,128)(2,1)S(1)} %bitcast.12), channel_id=1, replica_groups=mesh['row'=16,'col'=8] {'col'}, dimensions={0} | all-to-all | bytes 12582912 | tf_op jit(solution)/shard_map/all_to_all | solution.py:22
  158.1 4.2 reduce_sum.12
  162.2 0.3 copy.6
  162.5 5.8 %stack.2 = bf16[16,768,512]{1,2,0:T(8,128)(2,1)} broadcast(bf16[768,512]{0,1:T(8,128)(2,1)S(1)} %copy.6), dimensions={1,2} | broadcast | bytes 13369344 | tf_op jit(solution)/shard_map/stack | solution.py:9
  168.3 144.2 %all_to_all.11 = bf16[16,768,512]{1,2,0:T(8,128)(2,1)S(1)} all-to-all(bf16[16,768,512]{1,2,0:T(8,128)(2,1)} %stack.2), channel_id=1, replica_groups=mesh['row'=16,'col'=8] {'row'}, dimensions={0} | all-to-all | bytes 25165824 | tf_op jit(solution)/shard_map/all_to_all | solution.py:10
  312.5 0.0 copy-done
  312.5 9.2 %fusion = bf16[512,8192]{0,1:T(8,128)(2,1)} fusion(bf16[768,8192]{0,1:T(8,128)(2,1)S(1)} %bitcast.11, bf16[512,768]{1,0:T(8,128)(2,1)S(1)} %copy-done), kind=kOutput, calls=%fused_computation.1 | convolution fusion | flops 6446645248 | bytes 21757952 | tf_op jit(solution)/shard_map/dot_general | solution.py:38
  321.7 12.0 %copy.8 = bf16[512,8192]{1,0:T(8,128)(2,1)} copy(bf16[512,8192]{0,1:T(8,128)(2,1)} %fusion) | data formatting | bytes 16777216
  333.7 0.0 reduce-scatter.4.cloned.1.call-update
  333.7 111.2 %reduce-scatter.4.cloned.1.call-done = bf16[64,8192]{1,0:T(8,128)(2,1)} async-done(((bf16[512,8192]{1,0:T(8,128)(2,1)}), bf16[64,8192]{1,0:T(8,128)(2,1)}) %reduce-scatter.4.cloned.1.call-update) | async-done | bytes 1048592 | tf_op jit(solution)/shard_map/reduce_scatter | solution.py:39
Async XLA Ops:
  6.5 306.0 %copy-start = (bf16[512,768]{1,0:T(8,128)(2,1)S(1)}, bf16[512,768]{1,0:T(8,128)(2,1)}, u32[]{:S(2)}) copy-start(bf16[512,768]{1,0:T(8,128)(2,1)} %param.5) | copy-start | bytes 2359300
  6.5 62.0 %all-gather.2.cloned.1.call-start = ((), (), s32[]{:S(2)}) async-start(), calls=%async_computation.3 | async-start | bytes 10027008 | tf_op jit(solution)/shard_map/all_gather | solution.py:31
  7.3 437.7 %reduce-scatter.4.cloned.1.call-start = ((), (), s32[]{:S(2)}) async-start(), calls=%async_computation.4 | async-start | bytes 9437184 | tf_op jit(solution)/shard_map/reduce_scatter | solution.py:39
Sparse Core Ops, SparseCore 0:
  9.0 59.4 all-gather.1
  333.9 111.0 reduce-scatter.3
